TPU v7x, 256 devices: a whole 4x4x8 slice. The times are simulated.
256 devices in a mesh: op: 16 (over y, z_hi), right: 16 (over z_lo, x, core).
Axes of the slice: x: 4, y: 4, z: 8 (z_hi: 4, z_lo: 2; z = z_hi * 2 + z_lo), core: 2. Of those that a mesh axis runs over, the one named last changes fastest.
Arguments:
- psi: float32 [768, 16384], P('op', 'right'), may hold values from -6 to 6
- left_env: float32 [32, 768, 768], P('op', 'right'), may hold values from -0.078125 to 0.078125
- right_env: float32 [32, 16384, 1024], P('op', 'right'), may hold values from -0.1875 to 0.1875
- sector_lengths: int32 [4], replicated, may hold values from 128 to 384, as said below
- op_map: int32 [32, 4], replicated, may hold values from 0 to 3
Outputs:
- h_psi: float32 [768, 16384], P('op', 'right')
Inputs may be any that keep to these rules, and one draw needn't show every extreme that they name: `sector_lengths`: one sector, at a position that varies between draws, holds 384 states; every other sector holds 128.
All inputs are finite; a program needn't handle non-finite values.
Results may differ from a plain program's by a relative error of at most 0.0003.
Values sent between devices are 32-bit elements; how exact they have to be, the bound alone decides.
A program may use at most 64 MiB of HBM per device.

v0:
```python
import jax
import jax.numpy as jnp
from jax import lax
from jax.sharding import PartitionSpec as P


def on_device(psi, left_env, right_env, sector_lengths, op_map):
    terms = left_env.shape[0]
    width = left_env.shape[2]
    ends = jnp.cumsum(sector_lengths)
    places = jnp.arange(width, dtype=jnp.int32)
    sector = jnp.sum((places[:, None] >= ends[None, :]).astype(jnp.int32), axis=1)
    local_map = lax.dynamic_slice_in_dim(op_map, lax.axis_index("op") * terms, terms, 0)
    count = sector_lengths.shape[0]
    onehot = (sector[:, None] == jnp.arange(count, dtype=jnp.int32)[None, :]).astype(jnp.int32)
    targets = jnp.sum(onehot[None, :, :] * local_map[:, None, :], axis=2)
    whole = lax.all_gather(psi, "op", axis=0, tiled=True)
    inner = jnp.einsum("ac,wbc->wab", whole, right_env, precision=lax.Precision.HIGHEST)
    keep = (sector[None, :, None] == targets[:, None, :]).astype(jnp.float32)
    masked = lax.all_gather(left_env, "right", axis=1, tiled=True) * keep
    summed = jnp.einsum("wra,wab->rb", masked, inner, precision=lax.Precision.HIGHEST)
    return lax.psum_scatter(summed, "op", scatter_dimension=0, tiled=True)


def solution(mesh):
    in_specs = (P("op", "right"), P("op", "right", None), P("op", "right", None), P(), P())
    out_specs = P("op", "right")
    return jax.shard_map(
        on_device, mesh=mesh, in_specs=in_specs, out_specs=out_specs, check_vma=False
    )
```

profile of v0, /device:TPU:2, one launch (start us, length us, event | category | flops | bytes accessed | tf_op | source)
XLA Modules:
  0.0 239.5 jit_solution(2700261651093496640)
XLA Ops:
  6.5 0.0 copy-start
  6.5 0.0 all-gather.5.cloned.1.call-start
  6.5 0.7 all-gather.5.cloned.1.call-update
  7.3 0.0 all-gather.3.cloned.1.call-start
  7.3 0.7 all-gather.3.cloned.1.call-update
  8.0 0.0 reduce-scatter.2.cloned.1.call-start
  8.1 0.8 reduce-window.8
  8.9 0.0 copy-done
  8.9 0.1 constant_dynamic-slice_fusion
  9.0 0.1 copy.7
  9.1 0.1 convert_reduce_fusion
  9.2 0.1 multiply_reduce_fusion
  9.2 71.2 %all-gather.5.cloned.1.call-done = f32[768,1024]{1,0:T(8,128)} async-done(((f32[48,1024]{1,0:T(8,128)}), f32[768,1024]{1,0:T(8,128)}) %all-gather.5.cloned.1.call-update) | async-done | bytes 3145744 | tf_op jit(solution)/shard_map/all_gather | solution.py:17
  80.5 24.4 %fusion.4 = f32[2,1024,768]{1,2,0:T(8,128)} fusion(f32[2,1024,1024]{2,1,0:T(8,128)} %param.7, f32[768,1024]{1,0:T(8,128)} %all-gather.5.cloned.1.call-done), kind=kOutput, calls=%fused_computation.4 | convolution fusion | flops 19327352832 | bytes 17825792 | tf_op jit(solution)/shard_map/ac,wbc->wab/dot_general | solution.py:18
  104.8 16.0 %all-gather.3.cloned.1.call-done = f32[2,768,768]{2,1,0:T(8,128)} async-done(((f32[2,48,768]{2,1,0:T(8,128)}), f32[2,768,768]{2,1,0:T(8,128)}) %all-gather.3.cloned.1.call-update) | async-done | bytes 4718608 | tf_op jit(solution)/shard_map/all_gather | solution.py:20
  120.9 19.9 %fusion.9 = f32[768,1024]{1,0:T(8,128)} fusion(f32[2,1024,768]{1,2,0:T(8,128)} %fusion.4, f32[2,768,768]{2,1,0:T(8,128)} %all-gather.3.cloned.1.call-done, s32[2,768]{1,0:T(2,128)S(1)} %multiply_reduce_fusion, s32[768]{0:T(1024)S(1)} %convert_reduce_fusion), kind=kOutput, calls=%fused_computation.9 | convolution fusion | flops 14497873920 | bytes 14164992 | tf_op jit(solution)/shard_map/wra,wab->rb/dot_general | solution.py:21
  140.7 0.0 reduce-scatter.2.cloned.1.call-update
  140.8 92.2 %reduce-scatter.2.cloned.1.call-done = f32[48,1024]{1,0:T(8,128)} async-done(((f32[768,1024]{1,0:T(8,128)}), f32[48,1024]{1,0:T(8,128)}) %reduce-scatter.2.cloned.1.call-update) | async-done | bytes 196624 | tf_op jit(solution)/shard_map/reduce_scatter | solution.py:22
  (1 shorter events, 0.0 us)
Async XLA Ops:
  6.5 2.4 copy-start
  6.5 73.9 %all-gather.5.cloned.1.call-start = ((), (), s32[]{:S(2)}) async-start(), calls=%async_computation.2 | async-start | bytes 3342336 | tf_op jit(solution)/shard_map/all_gather | solution.py:17
  7.3 113.6 %all-gather.3.cloned.1.call-start = ((), (), s32[]{:S(2)}) async-start(), calls=%async_computation.1 | async-start | bytes 5013504 | tf_op jit(solution)/shard_map/all_gather | solution.py:20
  8.0 224.9 %reduce-scatter.2.cloned.1.call-start = ((), (), s32[]{:S(2)}) async-start(), calls=%async_computation.3 | async-start | bytes 3342336 | tf_op jit(solution)/shard_map/reduce_scatter | solution.py:22
Sparse Core Ops, SparseCore 0:
  9.8 70.5 all-gather.4
  82.3 38.5 all-gather.2
  140.9 92.0 reduce-scatter.1
where the time goes:
time: 240 us; the launch traced here: 239 us
  waiting for transfers between devices  181 us (75%)
  matrix products  44.3 us (18%)
  between operations  13.1 us (5%)
    reduce_scatter x1, waiting for transfers between devices, on_device(): return lax.psum_scatter(summed, 'op', scatter_dimension=0, tiled=True)  92.2 us
    all_gather x1, waiting for transfers between devices, on_device(): whole = lax.all_gather(psi, 'op', axis=0, tiled=True)  71.2 us
    dot_general x1, matrix products, on_device(): jnp.einsum('ac,wbc->wab', whole, right_env, precision=lax.Precision.HIGHEST)  24.4 us
    dot_general x1, matrix products, on_device(): jnp.einsum('wra,wab->rb', masked, inner, precision=lax.Precision.HIGHEST)  19.9 us
    all_gather x1, waiting for transfers between devices, on_device(): masked = lax.all_gather(left_env, 'right', axis=1, tiled=True) * keep  16 us
  transfers between devices with their start and end apart: 3, of which 3 were waited for; matrix products, arithmetic and copies ran while one was open for 11% of the time, Pallas kernels for 0%

commit v1 on v0

v1 whole, which is shorter than its diff:
```python
import jax
import jax.numpy as jnp
from jax import lax
from jax.experimental import pallas as pl
from jax.experimental.pallas import tpu as pltpu
from jax.sharding import PartitionSpec as P

MESH = pl.DeviceIdType.MESH
BF = jnp.bfloat16
F32 = jnp.float32
I32 = jnp.int32

R = 48
HALF = R // 2
STATES = 768
BLOCK = 1024
TILE = 256
TILES = BLOCK // TILE
GROUP = 4 * R
UNITS = 4 * TILES
LAG_FAR = 2
LAG_NEAR = 4
ROWS_NT = (((1,), (1,)), ((), ()))
ROWS_NN = (((1,), (0,)), ((), ()))


def mod4(v):
    return lax.rem(v, 4)


def dot(a, b, dims):
    return lax.dot_general(a, b, dims, preferred_element_type=F32)


def halves(v):
    hi = v.astype(BF)
    return hi, (v - hi.astype(F32)).astype(BF)


def step_of(k):
    return mod4(2 + k + lax.div(k * (k - 1), 2))


def kernel(
    psi, left, renv, lengths, op_map, out,
    pg, lg, raw, rh, rl, p2, ih, il, m2, q, far, near, zfar, znear,
    local_sem, prs, pzs, pys, lrs, lls, lxs, lcs, fs, fr, ns, nr, zfs, zfr, zns, znr,
):
    op, right = lax.axis_index("op"), lax.axis_index("right")
    y, h = lax.div(op, 4), mod4(op)
    l, x, c = lax.div(right, 8), mod4(lax.div(right, 2)), lax.rem(right, 2)
    yp, ym, yf = mod4(y + 1), mod4(y + 3), mod4(y + 2)
    hp, hm, hf = mod4(h + 1), mod4(h + 3), mod4(h + 2)
    xp, xm, xf = mod4(x + 1), mod4(x + 3), mod4(x + 2)
    lo = 1 - l

    def op_at(a, b):
        return a * 4 + b

    def right_at(a, b, d):
        return a * 8 + b * 2 + d

    to_yp, to_ym = (op_at(yp, h), right), (op_at(ym, h), right)
    to_hp, to_hm = (op_at(y, hp), right), (op_at(y, hm), right)
    to_xp, to_xm = (op, right_at(l, xp, c)), (op, right_at(l, xm, c))
    to_l, to_c = (op, right_at(lo, x, c)), (op, right_at(l, x, 1 - c))

    barrier = pltpu.get_barrier_semaphore()
    partners = (to_yp, to_ym, to_hp, to_hm, to_xp, to_xm, to_l, to_c)
    for device in partners:
        pl.semaphore_signal(barrier, inc=1, device_id=device, device_id_type=MESH)

    load_env = pltpu.make_async_copy(renv, raw, local_sem.at[0])
    load_psi = pltpu.make_async_copy(psi, pg.at[op], local_sem.at[1])
    load_left = pltpu.make_async_copy(left, lg.at[right], local_sem.at[2])
    load_psi.start()
    load_env.start()
    load_left.start()
    pl.semaphore_wait(barrier, len(partners))

    def send(src, dst, ssem, rsem, device):
        copy = pltpu.make_async_remote_copy(
            src_ref=src, dst_ref=dst, send_sem=ssem, recv_sem=rsem, device_id=device, device_id_type=MESH
        )
        copy.start()

    def arrived(dst, ssem, rsem, device):
        pltpu.make_async_remote_copy(
            src_ref=dst, dst_ref=dst, send_sem=ssem, recv_sem=rsem, device_id=device, device_id_type=MESH
        ).wait_recv()

    def piece(o, half):
        return pg.at[o, pl.ds(half * HALF, HALF)]

    counts = {"z": 0, "y": 0, "l": 0, "x": 0, "c": 0}
    psi_sems, left_sems = {"z": pzs, "y": pys}, {"l": lls, "x": lxs, "c": lcs}

    def psi_send(axis, o, half, device, src=None):
        sem = psi_sems[axis].at[counts[axis]]
        counts[axis] += 1
        dst = piece(o, half)
        send(dst if src is None else src.at[pl.ds(half * HALF, HALF)], dst, sem, prs.at[o, half], device)

    def psi_arrived(o, half):
        arrived(piece(o, half), pzs.at[0], prs.at[o, half], to_yp)

    def left_send(axis, r, w, device, src=None):
        sem = left_sems[axis].at[counts[axis]]
        counts[axis] += 1
        dst = lg.at[r, w]
        send(dst if src is None else src.at[w], dst, sem, lrs.at[r, w], device)

    def left_arrived(r, w):
        arrived(lg.at[r, w], lls.at[0], lrs.at[r, w], to_xp)

    psi_send("z", op, 0, to_hp, psi)
    psi_send("z", op, 1, to_hm, psi)
    psi_send("y", op, 0, to_yp, psi)
    psi_send("y", op, 1, to_ym, psi)
    psi_send("z", op, 1, to_hp, psi)
    psi_send("z", op, 0, to_hm, psi)
    psi_send("y", op, 1, to_yp, psi)
    psi_send("y", op, 0, to_ym, psi)
    for w in (0, 1):
        left_send("x", right, w, to_xp, left)
        left_send("x", right, 1 - w, to_xm, left)
    for w in (0, 1):
        left_send("c", right, w, to_c, left)

    def both_ways(o, half):
        psi_send("y", o, half, to_yp)
        psi_send("y", o, half, to_ym)

    def from_below(o_h):
        psi_arrived(op_at(ym, o_h), 0)
        psi_send("y", op_at(ym, o_h), 0, to_yp)

    def from_above(o_h):
        psi_arrived(op_at(yp, o_h), 1)
        psi_send("y", op_at(yp, o_h), 1, to_ym)

    def rest_of(o_h):
        psi_arrived(op_at(ym, o_h), 1)
        psi_arrived(op_at(yp, o_h), 0)
        psi_arrived(op_at(yf, o_h), 0)
        psi_arrived(op_at(yf, o_h), 1)

    def to_group(i, o_h):
        for a in range(4):
            hi, low = halves(pg[op_at(a, o_h)])
            p2[i, a * R:(a + 1) * R] = hi
            p2[i, GROUP + a * R:GROUP + (a + 1) * R] = low

    def left_on(r, w):
        left_arrived(r, w)
        left_send("c", r, w, to_c)

    def inner_tile(i, o_h, w, t):
        rows = pl.ds(pl.multiple_of(w * BLOCK + t * TILE, TILE), TILE)
        both = dot(p2[i], rh[rows, :], ROWS_NT)
        cross = dot(p2[i, :GROUP], rl[rows, :], ROWS_NT)
        hi, low = halves(both[:GROUP] + both[GROUP:] + cross)
        for a in range(4):
            at = pl.ds(pl.multiple_of(w * STATES + op_at(a, o_h) * R, 16), R)
            ih[t, at, :] = hi[a * R:(a + 1) * R]
            il[t, at, :] = low[a * R:(a + 1) * R]

    load_env.wait()

    def split_env(s, carry):
        rows = pl.ds(pl.multiple_of(s * 32, 32), 32)
        hi, low = halves(raw[rows, :])
        rh[rows, :] = hi
        rl[rows, :] = low
        return carry

    lax.fori_loop(0, 2 * BLOCK // 32, split_env, 0)
    load_psi.wait()

    from_below(h)
    from_above(h)
    psi_arrived(op_at(y, hm), 0)
    psi_send("z", op_at(y, hm), 0, to_hp)
    both_ways(op_at(y, hm), 0)
    psi_arrived(op_at(y, hp), 1)
    psi_send("z", op_at(y, hp), 1, to_hm)
    both_ways(op_at(y, hp), 1)
    left_send("l", right, 0, to_l, left)
    left_send("l", right, 1, to_l, left)
    left_arrived(right_at(l, xm, c), 0)
    left_send("x", right_at(l, xm, c), 0, to_xp)
    left_send("c", right_at(l, xm, c), 0, to_c)
    left_arrived(right_at(l, xp, c), 1)
    left_send("x", right_at(l, xp, c), 1, to_xm)
    left_send("c", right_at(l, xp, c), 1, to_c)
    rest_of(h)
    to_group(0, h)

    def second_halves():
        psi_arrived(op_at(y, hp), 0)
        both_ways(op_at(y, hp), 0)
        psi_arrived(op_at(y, hm), 1)
        both_ways(op_at(y, hm), 1)

    def ready(i, o_h):
        rest_of(o_h)
        to_group(i, o_h)

    def farthest(half):
        psi_arrived(op_at(y, hf), half)
        both_ways(op_at(y, hf), half)

    def left_across(w):
        r = right_at(lo, x, c)
        left_arrived(r, w)
        left_send("x", r, w, to_xp)
        left_send("x", r, w, to_xm)
        left_send("c", r, w, to_c)

    def left_turn():
        r = right_at(lo, xm, c)
        left_arrived(r, 0)
        left_send("x", r, 0, to_xp)
        left_send("c", r, 0, to_c)
        r = right_at(lo, xp, c)
        left_arrived(r, 1)
        left_send("x", r, 1, to_xm)
        left_send("c", r, 1, to_c)

    def left_pair(a, b, second):
        left_on(right_at(a, b[0], c), second[0])
        left_on(right_at(a, b[1], c), second[1])

    events = {
        1: [(left_pair, l, (xm, xp), (1, 0))],
        2: [(second_halves,)],
        3: [(from_above, hp), (from_below, hp)],
        4: [(left_pair, l, (xf, xf), (0, 1))],
        5: [(left_across, 0)],
        6: [(from_below, hm)],
        7: [(left_across, 1)],
        8: [(ready, 1, hp)],
        9: [(farthest, 0)],
        10: [(farthest, 1)],
        11: [(from_above, hm)],
        13: [(left_turn,)],
        15: [(left_pair, lo, (xm, xp), (1, 0))],
        16: [(ready, 2, hm)],
        18: [(from_below, hf)],
        19: [(from_above, hf)],
        21: [(left_pair, lo, (xf, xf), (0, 1))],
    }

    def gather_step(e, carry):
        for at, calls in events.items():
            @pl.when(e == at)
            def _(calls=calls):
                for call, *rest in calls:
                    call(*rest)

        i = lax.div(e, 8)
        o_h = mod4(h + i + lax.div(i, 2))
        inner_tile(i, o_h, lax.rem(lax.div(e, 4), 2), mod4(e))
        return carry

    lax.fori_loop(0, 24, gather_step, 0)

    load_left.wait()
    for a in range(2):
        for b in range(4):
            for w in range(2):
                left_arrived(right_at(a, b, 1 - c), w)

    ends = []
    total = 0
    for k in range(4):
        total = total + lengths[k]
        ends.append(total)

    def sector_of(place):
        s = jnp.zeros(place.shape, I32)
        for end in ends:
            s = s + (place >= end).astype(I32)
        return s

    column_sector = sector_of(lax.broadcasted_iota(I32, (R, STATES), 1))
    targets = []
    for w in range(2):
        target = jnp.full((R, STATES), -1, I32)
        for k in range(4):
            target = jnp.where(column_sector == k, op_map[k, 2 * op + w], target)
        targets.append(target)

    def mask_rows(r, carry):
        sector = sector_of(lax.broadcasted_iota(I32, (R, STATES), 0) + r * R)
        a, b = lax.div(r, 4), mod4(r)
        for w in range(2):
            hi, low = halves(jnp.where(sector == targets[w], lg[r, w], 0.0))
            columns = slice(w * STATES, (w + 1) * STATES)
            m2[b, pl.ds(pl.multiple_of(a * R, 16), R), columns] = hi
            m2[b, pl.ds(pl.multiple_of(GROUP + a * R, 16), R), columns] = low
        return carry

    lax.fori_loop(0, 16, mask_rows, 0)

    rest_of(hf)
    to_group(3, hf)

    def rows_at(u, a, half):
        return q.at[u, pl.ds(pl.multiple_of(a * R + half * HALF, 8), HALF)]

    def half_of(ref, half):
        return ref.at[pl.ds(half * HALF, HALF)]

    def multiply(u):
        t, k = lax.div(u, 4), mod4(u)

        @pl.when(k == 0)
        def _():
            def one(w, carry):
                inner_tile(3, hf, w, t)
                return carry

            lax.fori_loop(0, 2, one, 0)

        o_h = mod4(h + step_of(k))
        both = dot(m2[o_h], ih[t], ROWS_NN)
        cross = dot(m2[o_h, :GROUP], il[t], ROWS_NN)
        q[u] = both[:GROUP] + both[GROUP:] + cross
        send(rows_at(u, yf, 0), far.at[u, 0], fs.at[u, 0], fr.at[u, 0], to_yp)
        send(rows_at(u, yf, 1), far.at[u, 1], fs.at[u, 1], fr.at[u, 1], to_ym)
        send(rows_at(u, yp, 1), half_of(near.at[u, 0], 1), ns.at[u, 0, 1], nr.at[u, 0, 1], to_yp)
        send(rows_at(u, ym, 0), half_of(near.at[u, 1], 0), ns.at[u, 1, 0], nr.at[u, 1, 0], to_ym)

    def pass_on(u):
        arrived(far.at[u, 0], fs.at[u, 0], fr.at[u, 0], to_yp)
        at = rows_at(u, yp, 0)
        at[...] = at[...] + far[u, 0]
        send(at, half_of(near.at[u, 0], 0), ns.at[u, 0, 0], nr.at[u, 0, 0], to_yp)
        arrived(far.at[u, 1], fs.at[u, 1], fr.at[u, 1], to_ym)
        at = rows_at(u, ym, 1)
        at[...] = at[...] + far[u, 1]
        send(at, half_of(near.at[u, 1], 1), ns.at[u, 1, 1], nr.at[u, 1, 1], to_ym)

    def total_along_y(u):
        t, k = lax.div(u, 4), mod4(u)
        for d in range(2):
            for half in range(2):
                arrived(half_of(near.at[u, d], half), ns.at[u, d, half], nr.at[u, d, half], to_yp)
        at = q.at[u, pl.ds(pl.multiple_of(y * R, 16), R)]
        at[...] = at[...] + near[u, 0] + near[u, 1]

        @pl.when(k == 0)
        def _():
            send(rows_at(u, y, 0), zfar.at[t, 0], zfs.at[t, 0], zfr.at[t, 0], to_hp)
            send(rows_at(u, y, 1), zfar.at[t, 1], zfs.at[t, 1], zfr.at[t, 1], to_hm)

        @pl.when(k == 1)
        def _():
            send(rows_at(u, y, 0), half_of(znear.at[t, 1], 0), zns.at[t, 1, 0], znr.at[t, 1, 0], to_hm)

        @pl.when(k == 2)
        def _():
            send(rows_at(u, y, 1), half_of(znear.at[t, 0], 1), zns.at[t, 0, 1], znr.at[t, 0, 1], to_hp)

        @pl.when(k == 3)
        def _():
            arrived(zfar.at[t, 0], zfs.at[t, 0], zfr.at[t, 0], to_hp)
            up = rows_at(u - 1, y, 0)
            up[...] = up[...] + zfar[t, 0]
            send(up, half_of(znear.at[t, 0], 0), zns.at[t, 0, 0], znr.at[t, 0, 0], to_hp)
            arrived(zfar.at[t, 1], zfs.at[t, 1], zfr.at[t, 1], to_hm)
            down = rows_at(u - 2, y, 1)
            down[...] = down[...] + zfar[t, 1]
            send(down, half_of(znear.at[t, 1], 1), zns.at[t, 1, 1], znr.at[t, 1, 1], to_hm)

    def total_along_z(t):
        for d in range(2):
            for half in range(2):
                arrived(half_of(znear.at[t, d], half), zns.at[t, d, half], znr.at[t, d, half], to_hp)
        mine = q[4 * t + 3, pl.ds(pl.multiple_of(y * R, 16), R)]
        out[:, pl.ds(pl.multiple_of(t * TILE, TILE), TILE)] = mine + znear[t, 0] + znear[t, 1]

    def scatter_step(s, carry):
        @pl.when(s < UNITS)
        def _():
            multiply(s)

        @pl.when((s >= LAG_FAR) & (s < UNITS + LAG_FAR))
        def _():
            pass_on(s - LAG_FAR)

        v = s - LAG_NEAR

        @pl.when(v >= 0)
        def _():
            total_along_y(v)

        @pl.when((v >= 6) & (mod4(v) == 2))
        def _():
            total_along_z(lax.div(v - 6, 4))

        return carry

    lax.fori_loop(0, UNITS + LAG_NEAR, scatter_step, 0)
    total_along_z(TILES - 1)

    def sent_out(ref, sem):
        pltpu.make_async_remote_copy(
            src_ref=ref, dst_ref=ref, send_sem=sem, recv_sem=sem, device_id=to_yp, device_id_type=MESH
        ).wait_send()

    def all_out(u, carry):
        for d in range(2):
            sent_out(far.at[u, d], fs.at[u, d])
            for half in range(2):
                sent_out(half_of(near.at[u, d], half), ns.at[u, d, half])
        return carry

    lax.fori_loop(0, UNITS, all_out, 0)
    for sems in (pzs, pys):
        for n in range(sems.shape[0]):
            sent_out(pg.at[0, pl.ds(0, HALF)], sems.at[n])
    for sems in (lls, lxs, lcs):
        for n in range(sems.shape[0]):
            sent_out(lg.at[0, 0], sems.at[n])
    for t in range(TILES):
        for d in range(2):
            sent_out(zfar.at[t, d], zfs.at[t, d])
            for half in range(2):
                sent_out(half_of(znear.at[t, d], half), zns.at[t, d, half])


def on_device(psi, left_env, right_env, sector_lengths, op_map):
    dma = pltpu.SemaphoreType.DMA
    anywhere = pl.BlockSpec(memory_space=pl.ANY)
    scalars = pl.BlockSpec(memory_space=pltpu.SMEM)
    return pl.pallas_call(
        kernel,
        out_shape=jax.ShapeDtypeStruct((R, BLOCK), F32),
        in_specs=[anywhere, anywhere, anywhere, scalars, scalars],
        out_specs=pl.BlockSpec(memory_space=pltpu.VMEM),
        scratch_shapes=[
            pltpu.VMEM((16, R, BLOCK), F32),
            pltpu.VMEM((16, 2, R, STATES), F32),
            pltpu.VMEM((2 * BLOCK, BLOCK), F32),
            pltpu.VMEM((2 * BLOCK, BLOCK), BF),
            pltpu.VMEM((2 * BLOCK, BLOCK), BF),
            pltpu.VMEM((4, 2 * GROUP, BLOCK), BF),
            pltpu.VMEM((TILES, 2 * STATES, TILE), BF),
            pltpu.VMEM((TILES, 2 * STATES, TILE), BF),
            pltpu.VMEM((4, 2 * GROUP, 2 * STATES), BF),
            pltpu.VMEM((UNITS, GROUP, TILE), F32),
            pltpu.VMEM((UNITS, 2, HALF, TILE), F32),
            pltpu.VMEM((UNITS, 2, R, TILE), F32),
            pltpu.VMEM((TILES, 2, HALF, TILE), F32),
            pltpu.VMEM((TILES, 2, R, TILE), F32),
            dma((3,)),
            dma((16, 2)), dma((6,)), dma((24,)),
            dma((16, 2)), dma((2,)), dma((12,)), dma((16,)),
            dma((UNITS, 2)), dma((UNITS, 2)), dma((UNITS, 2, 2)), dma((UNITS, 2, 2)),
            dma((TILES, 2)), dma((TILES, 2)), dma((TILES, 2, 2)), dma((TILES, 2, 2)),
        ],
        compiler_params=pltpu.CompilerParams(
            collective_id=0, has_side_effects=True, vmem_limit_bytes=60 * 1024 * 1024
        ),
    )(psi, left_env, right_env.reshape(2 * BLOCK, BLOCK), sector_lengths, op_map.T)


def solution(mesh):
    in_specs = (P("op", "right"), P("op", "right", None), P("op", "right", None), P(), P())
    return jax.shard_map(
        on_device, mesh=mesh, in_specs=in_specs, out_specs=P("op", "right"), check_vma=False
    )
```

time: 240 us -> 90.6 us (0.38)
  waiting for transfers between devices: 181 us -> 0 us
  Pallas kernels: 0 us -> 88.2 us
  matrix products: 44.3 us -> 0 us
  between operations: 13.1 us -> 0.01 us
    reduce_scatter x1 -> x0, waiting for transfers between devices: 92.2 us -> none  [on_device(): return lax.psum_scatter(summed, 'op', scatter_dimension=0, tiled=True)]
    pallas_call x0 -> x1, Pallas kernels: none -> 88.2 us  [on_device(): pl.pallas_call(kernel, out_shape=jax.ShapeDtypeStruct((R, BLOCK), F32), i...]
    all_gather x2 -> x0, waiting for transfers between devices: 87.2 us -> none  [the longest x1 71.2 us: on_device(): whole = lax.all_gather(psi, 'op', axis=0, tiled=True)]
    dot_general x2 -> x0, matrix products: 44.3 us -> none  [the longest x1 24.4 us: on_device(): jnp.einsum('ac,wbc->wab', whole, right_env, precision=lax.Precision.HIGHEST)]
  transfers between devices with their start and end apart: 3 -> 0, of which waited for: 3 -> 0; matrix products, arithmetic and copies ran while one was open for 11% -> 0% of each run, Pallas kernels for 0% -> 0%
where the time goes in v1:
time: 90.6 us; the launch traced here: 89.9 us
  Pallas kernels  88.2 us (97%)
  local copies, waits for them, and re-layouts  1.62 us (2%)
    pallas_call x1, Pallas kernels, on_device(): pl.pallas_call(kernel, out_shape=jax.ShapeDtypeStruct((R, BLOCK), F32), i...  88.2 us

profile of v1, /device:TPU:2, one launch (start us, length us, event | category | flops | bytes accessed | tf_op | source)
XLA Modules:
  0.0 89.9 jit_solution(16127346556992286317)
XLA Ops:
  0.0 88.2 %shard_map.55 = f32[48,1024]{1,0:T(8,128)} custom-call(f32[48,1024]{1,0:T(8,128)} %psi.1, f32[2,48,768]{2,1,0:T(8,128)} %left.1, f32[2048,1024]{1,0:T(8,128)} %bitcast.2, s32[4]{0:T(128)} %lengths.1, s32[4,32]{1,0:T(4,128)} %bitcast.3), custom_call_target="tpu_custom_call" | custom-call | tf_op jit(solution)/shard_map/pallas_call | solution.py:438
  88.2 1.6 %copy.7 = f32[48,1024]{1,0:T(8,128)} copy(f32[48,1024]{1,0:T(8,128)} %shard_map.55) | data formatting | bytes 393216

commit v2 on v1

--- a/solution.py
+++ b/solution.py
@@ -19,7 +19,7 @@
 GROUP = 4 * R
 UNITS = 4 * TILES
 LAG_FAR = 2
-LAG_NEAR = 4
+LAG_NEAR = 5
 ROWS_NT = (((1,), (1,)), ((), ()))
 ROWS_NN = (((1,), (0,)), ((), ()))
 
@@ -43,7 +43,7 @@
 
 def kernel(
     psi, left, renv, lengths, op_map, out,
-    pg, lg, raw, rh, rl, p2, ih, il, m2, q, far, near, zfar, znear,
+    pg, lg, raw, rh, rl, p2, early, ih, il, m2, q, far, near, zfar, znear,
     local_sem, prs, pzs, pys, lrs, lls, lxs, lcs, fs, fr, ns, nr, zfs, zfr, zns, znr,
 ):
     op, right = lax.axis_index("op"), lax.axis_index("right")
@@ -145,9 +145,10 @@
         psi_arrived(op_at(yf, o_h), 0)
         psi_arrived(op_at(yf, o_h), 1)
 
-    def to_group(i, o_h):
+    def to_group(i, first, second):
         for a in range(4):
-            hi, low = halves(pg[op_at(a, o_h)])
+            rows = jnp.concatenate([pg[op_at(a, first), :HALF], pg[op_at(a, second), HALF:]], axis=0)
+            hi, low = halves(rows)
             p2[i, a * R:(a + 1) * R] = hi
             p2[i, GROUP + a * R:GROUP + (a + 1) * R] = low
 
@@ -155,11 +156,14 @@
         left_arrived(r, w)
         left_send("c", r, w, to_c)
 
-    def inner_tile(i, o_h, w, t):
+    def inner_tile(i, w, t):
         rows = pl.ds(pl.multiple_of(w * BLOCK + t * TILE, TILE), TILE)
         both = dot(p2[i], rh[rows, :], ROWS_NT)
         cross = dot(p2[i, :GROUP], rl[rows, :], ROWS_NT)
-        hi, low = halves(both[:GROUP] + both[GROUP:] + cross)
+        return both[:GROUP] + both[GROUP:] + cross
+
+    def keep_inner(v, o_h, w, t):
+        hi, low = halves(v)
         for a in range(4):
             at = pl.ds(pl.multiple_of(w * STATES + op_at(a, o_h) * R, 16), R)
             ih[t, at, :] = hi[a * R:(a + 1) * R]
@@ -194,7 +198,7 @@
     left_send("x", right_at(l, xp, c), 1, to_xm)
     left_send("c", right_at(l, xp, c), 1, to_c)
     rest_of(h)
-    to_group(0, h)
+    to_group(0, h, h)
 
     def second_halves():
         psi_arrived(op_at(y, hp), 0)
@@ -202,9 +206,17 @@
         psi_arrived(op_at(y, hm), 1)
         both_ways(op_at(y, hm), 1)
 
-    def ready(i, o_h):
-        rest_of(o_h)
-        to_group(i, o_h)
+    def first_pairs():
+        for o_h, half in ((hm, 0), (hp, 1)):
+            psi_arrived(op_at(ym if half else yp, o_h), half)
+            psi_arrived(op_at(yf, o_h), half)
+        to_group(1, hm, hp)
+
+    def second_pairs():
+        for o_h, half in ((hp, 0), (hm, 1)):
+            psi_arrived(op_at(ym if half else yp, o_h), half)
+            psi_arrived(op_at(yf, o_h), half)
+        to_group(2, hp, hm)
 
     def farthest(half):
         psi_arrived(op_at(y, hf), half)
@@ -232,23 +244,19 @@
         left_on(right_at(a, b[1], c), second[1])
 
     events = {
-        1: [(left_pair, l, (xm, xp), (1, 0))],
-        2: [(second_halves,)],
-        3: [(from_above, hp), (from_below, hp)],
-        4: [(left_pair, l, (xf, xf), (0, 1))],
-        5: [(left_across, 0)],
-        6: [(from_below, hm)],
-        7: [(left_across, 1)],
-        8: [(ready, 1, hp)],
-        9: [(farthest, 0)],
-        10: [(farthest, 1)],
-        11: [(from_above, hm)],
-        13: [(left_turn,)],
-        15: [(left_pair, lo, (xm, xp), (1, 0))],
-        16: [(ready, 2, hm)],
-        18: [(from_below, hf)],
-        19: [(from_above, hf)],
-        21: [(left_pair, lo, (xf, xf), (0, 1))],
+        3: [(left_pair, l, (xm, xp), (1, 0))],
+        4: [(second_halves,)],
+        5: [(from_above, hp), (from_below, hm)],
+        7: [(left_pair, l, (xf, xf), (0, 1))],
+        8: [
+            (farthest, 0), (farthest, 1), (left_across, 0), (from_below, hp), (from_above, hm),
+            (left_across, 1), (first_pairs,),
+        ],
+        11: [(left_turn,)],
+        13: [(from_below, hf), (from_above, hf)],
+        16: [(second_pairs,)],
+        18: [(left_pair, lo, (xm, xp), (1, 0))],
+        22: [(left_pair, lo, (xf, xf), (0, 1))],
     }
 
     def gather_step(e, carry):
@@ -258,9 +266,25 @@
                 for call, *rest in calls:
                     call(*rest)
 
-        i = lax.div(e, 8)
-        o_h = mod4(h + i + lax.div(i, 2))
-        inner_tile(i, o_h, lax.rem(lax.div(e, 4), 2), mod4(e))
+        i, n = lax.div(e, 8), lax.rem(e, 8)
+        w, t = lax.div(n, 4), mod4(n)
+        v = inner_tile(i, w, t)
+
+        @pl.when(i == 0)
+        def _():
+            keep_inner(v, h, w, t)
+
+        @pl.when(i == 1)
+        def _():
+            early[n] = v
+
+        @pl.when(i == 2)
+        def _():
+            before = early[n]
+            first = lax.rem(lax.broadcasted_iota(I32, (GROUP, TILE), 0), R) < HALF
+            keep_inner(jnp.where(first, before, v), hm, w, t)
+            keep_inner(jnp.where(first, v, before), hp, w, t)
+
         return carry
 
     lax.fori_loop(0, 24, gather_step, 0)
@@ -304,7 +328,7 @@
     lax.fori_loop(0, 16, mask_rows, 0)
 
     rest_of(hf)
-    to_group(3, hf)
+    to_group(3, hf, hf)
 
     def rows_at(u, a, half):
         return q.at[u, pl.ds(pl.multiple_of(a * R + half * HALF, 8), HALF)]
@@ -312,13 +336,19 @@
     def half_of(ref, half):
         return ref.at[pl.ds(half * HALF, HALF)]
 
+    def place_of(u):
+        late = lax.div(u, 2 * TILES)
+        k = (1 - late) * lax.rem(u, 2) + late * lax.div(u, TILES)
+        t = (1 - late) * lax.div(u, 2) + late * lax.rem(u, TILES)
+        return k, t
+
     def multiply(u):
-        t, k = lax.div(u, 4), mod4(u)
+        k, t = place_of(u)
 
         @pl.when(k == 0)
         def _():
             def one(w, carry):
-                inner_tile(3, hf, w, t)
+                keep_inner(inner_tile(3, w, t), hf, w, t)
                 return carry
 
             lax.fori_loop(0, 2, one, 0)
@@ -343,7 +373,7 @@
         send(at, half_of(near.at[u, 1], 1), ns.at[u, 1, 1], nr.at[u, 1, 1], to_ym)
 
     def total_along_y(u):
-        t, k = lax.div(u, 4), mod4(u)
+        k, t = place_of(u)
         for d in range(2):
             for half in range(2):
                 arrived(half_of(near.at[u, d], half), ns.at[u, d, half], nr.at[u, d, half], to_yp)
@@ -362,24 +392,21 @@
         @pl.when(k == 2)
         def _():
             send(rows_at(u, y, 1), half_of(znear.at[t, 0], 1), zns.at[t, 0, 1], znr.at[t, 0, 1], to_hp)
-
-        @pl.when(k == 3)
-        def _():
+            arrived(zfar.at[t, 1], zfs.at[t, 1], zfr.at[t, 1], to_hm)
+            down = rows_at(2 * t + 1, y, 1)
+            down[...] = down[...] + zfar[t, 1]
+            send(down, half_of(znear.at[t, 1], 1), zns.at[t, 1, 1], znr.at[t, 1, 1], to_hm)
             arrived(zfar.at[t, 0], zfs.at[t, 0], zfr.at[t, 0], to_hp)
-            up = rows_at(u - 1, y, 0)
+            up = rows_at(u, y, 0)
             up[...] = up[...] + zfar[t, 0]
             send(up, half_of(znear.at[t, 0], 0), zns.at[t, 0, 0], znr.at[t, 0, 0], to_hp)
-            arrived(zfar.at[t, 1], zfs.at[t, 1], zfr.at[t, 1], to_hm)
-            down = rows_at(u - 2, y, 1)
-            down[...] = down[...] + zfar[t, 1]
-            send(down, half_of(znear.at[t, 1], 1), zns.at[t, 1, 1], znr.at[t, 1, 1], to_hm)
-
-    def total_along_z(t):
-        for d in range(2):
-            for half in range(2):
-                arrived(half_of(znear.at[t, d], half), zns.at[t, d, half], znr.at[t, d, half], to_hp)
-        mine = q[4 * t + 3, pl.ds(pl.multiple_of(y * R, 16), R)]
-        out[:, pl.ds(pl.multiple_of(t * TILE, TILE), TILE)] = mine + znear[t, 0] + znear[t, 1]
+
+        @pl.when(k == 3)
+        def _():
+            for d in range(2):
+                for half in range(2):
+                    arrived(half_of(znear.at[t, d], half), zns.at[t, d, half], znr.at[t, d, half], to_hp)
+            out[:, pl.ds(pl.multiple_of(t * TILE, TILE), TILE)] = at[...] + znear[t, 0] + znear[t, 1]
 
     def scatter_step(s, carry):
         @pl.when(s < UNITS)
@@ -396,14 +423,9 @@
         def _():
             total_along_y(v)
 
-        @pl.when((v >= 6) & (mod4(v) == 2))
-        def _():
-            total_along_z(lax.div(v - 6, 4))
-
         return carry
 
     lax.fori_loop(0, UNITS + LAG_NEAR, scatter_step, 0)
-    total_along_z(TILES - 1)
 
     def sent_out(ref, sem):
         pltpu.make_async_remote_copy(
@@ -447,6 +469,7 @@
             pltpu.VMEM((2 * BLOCK, BLOCK), BF),
             pltpu.VMEM((2 * BLOCK, BLOCK), BF),
             pltpu.VMEM((4, 2 * GROUP, BLOCK), BF),
+            pltpu.VMEM((2 * TILES, GROUP, TILE), F32),
             pltpu.VMEM((TILES, 2 * STATES, TILE), BF),
             pltpu.VMEM((TILES, 2 * STATES, TILE), BF),
             pltpu.VMEM((4, 2 * GROUP, 2 * STATES), BF),

time: 90.6 us -> 85.2 us (0.940)
  Pallas kernels: 88.2 us -> 83.4 us
    pallas_call x1, Pallas kernels: 88.2 us -> 83.4 us  [on_device(): pl.pallas_call(kernel, out_shape=jax.ShapeDtypeStruct((R, BLOCK), F32), i...]
where the time goes in v2:
time: 85.2 us; the launch traced here: 85.1 us
  Pallas kernels  83.4 us (98%)
  local copies, waits for them, and re-layouts  1.62 us (2%)
    pallas_call x1, Pallas kernels, on_device(): pl.pallas_call(kernel, out_shape=jax.ShapeDtypeStruct((R, BLOCK), F32), i...  83.4 us

profile of v2, /device:TPU:2, one launch (start us, length us, event | category | flops | bytes accessed | tf_op | source)
XLA Modules:
  0.0 85.1 jit_solution(8206034314146210706)
XLA Ops:
  0.0 83.4 %shard_map.55 = f32[48,1024]{1,0:T(8,128)} custom-call(f32[48,1024]{1,0:T(8,128)} %psi.1, f32[2,48,768]{2,1,0:T(8,128)} %left.1, f32[2048,1024]{1,0:T(8,128)} %bitcast.2, s32[4]{0:T(128)} %lengths.1, s32[4,32]{1,0:T(4,128)} %bitcast.3), custom_call_target="tpu_custom_call" | custom-call | tf_op jit(solution)/shard_map/pallas_call | solution.py:460
  83.4 1.6 %copy.7 = f32[48,1024]{1,0:T(8,128)} copy(f32[48,1024]{1,0:T(8,128)} %shard_map.55) | data formatting | bytes 393216

commit v3 on v2

--- a/solution.py
+++ b/solution.py
@@ -18,8 +18,8 @@
 TILES = BLOCK // TILE
 GROUP = 4 * R
 UNITS = 4 * TILES
-LAG_FAR = 2
-LAG_NEAR = 5
+LAG_FAR = 4
+LAG_NEAR = 8
 ROWS_NT = (((1,), (1,)), ((), ()))
 ROWS_NN = (((1,), (0,)), ((), ()))
 
@@ -43,7 +43,7 @@
 
 def kernel(
     psi, left, renv, lengths, op_map, out,
-    pg, lg, raw, rh, rl, p2, early, ih, il, m2, q, far, near, zfar, znear,
+    pg, lg, raw, rh, rl, p2, last, early, ih, il, m2, q, far, near, zfar, znear,
     local_sem, prs, pzs, pys, lrs, lls, lxs, lcs, fs, fr, ns, nr, zfs, zfr, zns, znr,
 ):
     op, right = lax.axis_index("op"), lax.axis_index("right")
@@ -145,22 +145,22 @@
         psi_arrived(op_at(yf, o_h), 0)
         psi_arrived(op_at(yf, o_h), 1)
 
-    def to_group(i, first, second):
+    def to_group(ref, size, at, first, second):
         for a in range(4):
             rows = jnp.concatenate([pg[op_at(a, first), :HALF], pg[op_at(a, second), HALF:]], axis=0)
             hi, low = halves(rows)
-            p2[i, a * R:(a + 1) * R] = hi
-            p2[i, GROUP + a * R:GROUP + (a + 1) * R] = low
+            ref[at + a * R:at + (a + 1) * R] = hi
+            ref[size + at + a * R:size + at + (a + 1) * R] = low
 
     def left_on(r, w):
         left_arrived(r, w)
         left_send("c", r, w, to_c)
 
-    def inner_tile(i, w, t):
+    def inner_tile(ref, size, w, t):
         rows = pl.ds(pl.multiple_of(w * BLOCK + t * TILE, TILE), TILE)
-        both = dot(p2[i], rh[rows, :], ROWS_NT)
-        cross = dot(p2[i, :GROUP], rl[rows, :], ROWS_NT)
-        return both[:GROUP] + both[GROUP:] + cross
+        both = dot(ref[...], rh[rows, :], ROWS_NT)
+        cross = dot(ref[:size], rl[rows, :], ROWS_NT)
+        return both[:size] + both[size:] + cross
 
     def keep_inner(v, o_h, w, t):
         hi, low = halves(v)
@@ -169,6 +169,44 @@
             ih[t, at, :] = hi[a * R:(a + 1) * R]
             il[t, at, :] = low[a * R:(a + 1) * R]
 
+    ends = []
+    total = 0
+    for k in range(4):
+        total = total + lengths[k]
+        ends.append(total)
+
+    def sector_of(place):
+        s = jnp.zeros(place.shape, I32)
+        for end in ends:
+            s = s + (place >= end).astype(I32)
+        return s
+
+    column_sector = sector_of(lax.broadcasted_iota(I32, (R, STATES), 1))
+    targets = []
+    for w in range(2):
+        target = jnp.full((R, STATES), -1, I32)
+        for k in range(4):
+            target = jnp.where(column_sector == k, op_map[k, 2 * op + w], target)
+        targets.append(target)
+
+    def mask_from(side):
+        for b in range(4):
+            for w in range(2):
+                left_arrived(right_at(side, b, 1 - c), w)
+
+        def mask_rows(n, carry):
+            r = side * 8 + n
+            sector = sector_of(lax.broadcasted_iota(I32, (R, STATES), 0) + r * R)
+            a, b = lax.div(r, 4), mod4(r)
+            for w in range(2):
+                hi, low = halves(jnp.where(sector == targets[w], lg[r, w], 0.0))
+                columns = slice(w * STATES, (w + 1) * STATES)
+                m2[b, pl.ds(pl.multiple_of(a * R, 16), R), columns] = hi
+                m2[b, pl.ds(pl.multiple_of(GROUP + a * R, 16), R), columns] = low
+            return carry
+
+        lax.fori_loop(0, 8, mask_rows, 0)
+
     load_env.wait()
 
     def split_env(s, carry):
@@ -180,6 +218,7 @@
 
     lax.fori_loop(0, 2 * BLOCK // 32, split_env, 0)
     load_psi.wait()
+    load_left.wait()
 
     from_below(h)
     from_above(h)
@@ -198,7 +237,7 @@
     left_send("x", right_at(l, xp, c), 1, to_xm)
     left_send("c", right_at(l, xp, c), 1, to_c)
     rest_of(h)
-    to_group(0, h, h)
+    to_group(p2.at[0], GROUP, 0, h, h)
 
     def second_halves():
         psi_arrived(op_at(y, hp), 0)
@@ -210,13 +249,13 @@
         for o_h, half in ((hm, 0), (hp, 1)):
             psi_arrived(op_at(ym if half else yp, o_h), half)
             psi_arrived(op_at(yf, o_h), half)
-        to_group(1, hm, hp)
+        to_group(p2.at[1], GROUP, 0, hm, hp)
 
     def second_pairs():
         for o_h, half in ((hp, 0), (hm, 1)):
             psi_arrived(op_at(ym if half else yp, o_h), half)
             psi_arrived(op_at(yf, o_h), half)
-        to_group(2, hp, hm)
+        to_group(last, 2 * GROUP, 0, hp, hm)
 
     def farthest(half):
         psi_arrived(op_at(y, hf), half)
@@ -250,13 +289,10 @@
         7: [(left_pair, l, (xf, xf), (0, 1))],
         8: [
             (farthest, 0), (farthest, 1), (left_across, 0), (from_below, hp), (from_above, hm),
-            (left_across, 1), (first_pairs,),
+            (left_across, 1), (mask_from, l), (first_pairs,),
         ],
         11: [(left_turn,)],
         13: [(from_below, hf), (from_above, hf)],
-        16: [(second_pairs,)],
-        18: [(left_pair, lo, (xm, xp), (1, 0))],
-        22: [(left_pair, lo, (xf, xf), (0, 1))],
     }
 
     def gather_step(e, carry):
@@ -268,7 +304,7 @@
 
         i, n = lax.div(e, 8), lax.rem(e, 8)
         w, t = lax.div(n, 4), mod4(n)
-        v = inner_tile(i, w, t)
+        v = inner_tile(p2.at[i], GROUP, w, t)
 
         @pl.when(i == 0)
         def _():
@@ -278,57 +314,17 @@
         def _():
             early[n] = v
 
-        @pl.when(i == 2)
-        def _():
-            before = early[n]
-            first = lax.rem(lax.broadcasted_iota(I32, (GROUP, TILE), 0), R) < HALF
-            keep_inner(jnp.where(first, before, v), hm, w, t)
-            keep_inner(jnp.where(first, v, before), hp, w, t)
-
         return carry
 
-    lax.fori_loop(0, 24, gather_step, 0)
-
-    load_left.wait()
-    for a in range(2):
-        for b in range(4):
-            for w in range(2):
-                left_arrived(right_at(a, b, 1 - c), w)
-
-    ends = []
-    total = 0
-    for k in range(4):
-        total = total + lengths[k]
-        ends.append(total)
-
-    def sector_of(place):
-        s = jnp.zeros(place.shape, I32)
-        for end in ends:
-            s = s + (place >= end).astype(I32)
-        return s
-
-    column_sector = sector_of(lax.broadcasted_iota(I32, (R, STATES), 1))
-    targets = []
-    for w in range(2):
-        target = jnp.full((R, STATES), -1, I32)
-        for k in range(4):
-            target = jnp.where(column_sector == k, op_map[k, 2 * op + w], target)
-        targets.append(target)
-
-    def mask_rows(r, carry):
-        sector = sector_of(lax.broadcasted_iota(I32, (R, STATES), 0) + r * R)
-        a, b = lax.div(r, 4), mod4(r)
-        for w in range(2):
-            hi, low = halves(jnp.where(sector == targets[w], lg[r, w], 0.0))
-            columns = slice(w * STATES, (w + 1) * STATES)
-            m2[b, pl.ds(pl.multiple_of(a * R, 16), R), columns] = hi
-            m2[b, pl.ds(pl.multiple_of(GROUP + a * R, 16), R), columns] = low
-        return carry
-
-    lax.fori_loop(0, 16, mask_rows, 0)
+    lax.fori_loop(0, 16, gather_step, 0)
+    second_pairs()
+    left_pair(lo, (xm, xp), (1, 0))
+    left_pair(lo, (xf, xf), (0, 1))
+
+    mask_from(lo)
 
     rest_of(hf)
-    to_group(3, hf, hf)
+    to_group(last, 2 * GROUP, GROUP, hf, hf)
 
     def rows_at(u, a, half):
         return q.at[u, pl.ds(pl.multiple_of(a * R + half * HALF, 8), HALF)]
@@ -337,9 +333,9 @@
         return ref.at[pl.ds(half * HALF, HALF)]
 
     def place_of(u):
-        late = lax.div(u, 2 * TILES)
-        k = (1 - late) * lax.rem(u, 2) + late * lax.div(u, TILES)
-        t = (1 - late) * lax.div(u, 2) + late * lax.rem(u, TILES)
+        late = lax.div(u, 3 * TILES)
+        k = (1 - late) * lax.rem(u, 3) + late * 3
+        t = (1 - late) * lax.div(u, 3) + late * lax.rem(u, 3 * TILES)
         return k, t
 
     def multiply(u):
@@ -348,7 +344,12 @@
         @pl.when(k == 0)
         def _():
             def one(w, carry):
-                keep_inner(inner_tile(3, w, t), hf, w, t)
+                v = inner_tile(last, 2 * GROUP, w, t)
+                keep_inner(v[GROUP:], hf, w, t)
+                before, after = early[w * TILES + t], v[:GROUP]
+                first = lax.rem(lax.broadcasted_iota(I32, (GROUP, TILE), 0), R) < HALF
+                keep_inner(jnp.where(first, before, after), hm, w, t)
+                keep_inner(jnp.where(first, after, before), hp, w, t)
                 return carry
 
             lax.fori_loop(0, 2, one, 0)
@@ -372,6 +373,16 @@
         at[...] = at[...] + far[u, 1]
         send(at, half_of(near.at[u, 1], 1), ns.at[u, 1, 1], nr.at[u, 1, 1], to_ym)
 
+    def pass_on_z(t):
+        arrived(zfar.at[t, 1], zfs.at[t, 1], zfr.at[t, 1], to_hm)
+        down = rows_at(3 * t + 1, y, 1)
+        down[...] = down[...] + zfar[t, 1]
+        send(down, half_of(znear.at[t, 1], 1), zns.at[t, 1, 1], znr.at[t, 1, 1], to_hm)
+        arrived(zfar.at[t, 0], zfs.at[t, 0], zfr.at[t, 0], to_hp)
+        up = rows_at(3 * t + 2, y, 0)
+        up[...] = up[...] + zfar[t, 0]
+        send(up, half_of(znear.at[t, 0], 0), zns.at[t, 0, 0], znr.at[t, 0, 0], to_hp)
+
     def total_along_y(u):
         k, t = place_of(u)
         for d in range(2):
@@ -392,14 +403,6 @@
         @pl.when(k == 2)
         def _():
             send(rows_at(u, y, 1), half_of(znear.at[t, 0], 1), zns.at[t, 0, 1], znr.at[t, 0, 1], to_hp)
-            arrived(zfar.at[t, 1], zfs.at[t, 1], zfr.at[t, 1], to_hm)
-            down = rows_at(2 * t + 1, y, 1)
-            down[...] = down[...] + zfar[t, 1]
-            send(down, half_of(znear.at[t, 1], 1), zns.at[t, 1, 1], znr.at[t, 1, 1], to_hm)
-            arrived(zfar.at[t, 0], zfs.at[t, 0], zfr.at[t, 0], to_hp)
-            up = rows_at(u, y, 0)
-            up[...] = up[...] + zfar[t, 0]
-            send(up, half_of(znear.at[t, 0], 0), zns.at[t, 0, 0], znr.at[t, 0, 0], to_hp)
 
         @pl.when(k == 3)
         def _():
@@ -418,6 +421,10 @@
             pass_on(s - LAG_FAR)
 
         v = s - LAG_NEAR
+
+        @pl.when((v >= 3) & (v <= 3 * TILES) & (lax.rem(v, 3) == 0))
+        def _():
+            pass_on_z(lax.div(v, 3) - 1)
 
         @pl.when(v >= 0)
         def _():
@@ -468,7 +475,8 @@
             pltpu.VMEM((2 * BLOCK, BLOCK), F32),
             pltpu.VMEM((2 * BLOCK, BLOCK), BF),
             pltpu.VMEM((2 * BLOCK, BLOCK), BF),
-            pltpu.VMEM((4, 2 * GROUP, BLOCK), BF),
+            pltpu.VMEM((2, 2 * GROUP, BLOCK), BF),
+            pltpu.VMEM((4 * GROUP, BLOCK), BF),
             pltpu.VMEM((2 * TILES, GROUP, TILE), F32),
             pltpu.VMEM((TILES, 2 * STATES, TILE), BF),
             pltpu.VMEM((TILES, 2 * STATES, TILE), BF),

time: 85.2 us -> 81.1 us (0.952)
  Pallas kernels: 83.4 us -> 79.1 us
    pallas_call x1, Pallas kernels: 83.4 us -> 79.1 us  [on_device(): pl.pallas_call(kernel, out_shape=jax.ShapeDtypeStruct((R, BLOCK), F32), i...]
where the time goes in v3:
time: 81.1 us; the launch traced here: 80.8 us
  Pallas kernels  79.1 us (98%)
  local copies, waits for them, and re-layouts  1.62 us (2%)
    pallas_call x1, Pallas kernels, on_device(): pl.pallas_call(kernel, out_shape=jax.ShapeDtypeStruct((R, BLOCK), F32), i...  79.1 us

profile of v3, /device:TPU:2, one launch (start us, length us, event | category | flops | bytes accessed | tf_op | source)
XLA Modules:
  0.0 80.8 jit_solution(12697140425609088808)
XLA Ops:
  0.0 79.1 %shard_map.55 = f32[48,1024]{1,0:T(8,128)} custom-call(f32[48,1024]{1,0:T(8,128)} %psi.1, f32[2,48,768]{2,1,0:T(8,128)} %left.1, f32[2048,1024]{1,0:T(8,128)} %bitcast.2, s32[4]{0:T(128)} %lengths.1, s32[4,32]{1,0:T(4,128)} %bitcast.3), custom_call_target="tpu_custom_call" | custom-call | tf_op jit(solution)/shard_map/pallas_call | solution.py:467
  79.2 1.6 %copy.7 = f32[48,1024]{1,0:T(8,128)} copy(f32[48,1024]{1,0:T(8,128)} %shard_map.55) | data formatting | bytes 393216
